TPU v7x, 32 devices: a whole 2x2x4 slice. The times are simulated.
32 devices in a mesh: depth: 2 (over core), rows: 2 (over x), shots: 8 (over z, y).
Axes of the slice: x: 2, y: 2, z: 4, core: 2. Of those that a mesh axis runs over, the one named last changes fastest.
Arguments:
- sources: float32 [2, 2, 1024, 1024], P('depth', None, 'rows', 'shots'), may hold values from -6 to 6
- factor: float32 [2, 2, 1024, 1024], P('depth', None, ('rows', 'shots')), may hold values from -0.09375 to 0.09375
- block_mask: int32 [2, 2, 8, 8], P('depth'), may hold values 0 or 1
- inverse_diagonal: float32 [2, 2, 1024, 1024], P('depth', None, None, 'rows'), may hold values from -1.2 to 1.2, as said below
Outputs:
- solution: float32 [2, 2, 1024, 1024], P('depth', None, 'rows', 'shots')
Inputs may be any that keep to these rules, and one draw needn't show every extreme that they name: Each block inverse_diagonal[d, m] is lower triangular with diagonal entries between 0.8 and 1.2.
All inputs are finite; a program needn't handle non-finite values. No bound on the sum of `block_mask` on one device may be relied on, other than what follows from the above.
Results may differ from a plain program's by a relative error of at most 0.0001.
Values sent between devices are 32-bit elements; how exact they have to be, the bound alone decides.
No kernel may reach another device: no remote copies, remote signals or barrier semaphores. Data moves between devices by JAX's collectives and lax.ppermute only.
A program may use at most 64 MiB of HBM per device.

v0:
```python
import jax
import jax.numpy as jnp
from jax import lax
from jax.sharding import PartitionSpec as P


def mask_rows(factor_rows, block_mask, row_start, block_size):
    row_total = factor_rows.shape[1]
    block_count = block_mask.shape[3]
    row_blocks = (row_start + jnp.arange(row_total, dtype=jnp.int32)) // block_size
    row_select = (row_blocks[:, None] == jnp.arange(block_count, dtype=jnp.int32)[None, :]).astype(
        jnp.float32
    )
    row_masks = jnp.einsum("rk,pkc->prc", row_select, block_mask[0].astype(jnp.float32))
    return factor_rows * jnp.repeat(row_masks, block_size, axis=2)


def group_reduce(partial_value):
    summed = lax.psum_scatter(partial_value, "depth", scatter_dimension=0, tiled=True)
    return summed[0]


def group_collect(spread):
    every_rows = lax.all_gather(spread[None], "depth", axis=0, tiled=True)
    return every_rows


def invert_level(inverse_block, own_rows):
    inverse_term = jnp.dot(
        inverse_block, own_rows, precision=lax.Precision.HIGHEST, preferred_element_type=jnp.float32
    )
    return lax.psum(inverse_term, "rows")


def per_device(sources, factor, block_mask, inverse_diagonal):
    depth_count = lax.axis_size("depth")
    tree_height = depth_count.bit_length() - 1
    level_count = tree_height + 1
    rows_index = lax.axis_index("rows")
    full_width = factor.shape[3]
    block_count = block_mask.shape[3]
    block_size = full_width // block_count
    highest = lax.Precision.HIGHEST
    front_factor = lax.all_gather(factor[0], "shots", axis=1, tiled=True)
    front_count = front_factor.shape[1]
    masked = mask_rows(front_factor, block_mask, rows_index * front_count, block_size)
    solved = []
    for tier_index in range(level_count):
        own_rows = sources[0, tier_index]
        if tier_index > 0:
            group_size = 2**tier_index
            factor_tiles = masked.reshape(tier_index, group_size, front_count, full_width)
            lower_solved = jnp.stack(solved[:tier_index])
            partial_value = jnp.einsum(
                "lgrs,lsn->grn",
                factor_tiles,
                lower_solved,
                precision=highest,
                preferred_element_type=jnp.float32,
            )
            reduced = group_reduce(partial_value)
            own_rows = own_rows - reduced
        full_rows = invert_level(inverse_diagonal[0, tier_index], own_rows)
        solved.append(full_rows)
    answers = [None] * level_count
    collected = {}
    for tier_index in reversed(range(level_count)):
        target = solved[tier_index]
        if tier_index < tree_height:
            factor_tiles = masked
            transposed = jnp.einsum(
                "grs,grn->sn",
                factor_tiles,
                collected[1],
                precision=highest,
                preferred_element_type=jnp.float32,
            )
            own_columns = lax.psum(transposed, "rows")
            target = target - own_columns
        answer = lax.dot_general(
            inverse_diagonal[0, tier_index],
            target,
            (((0,), (0,)), ((), ())),
            precision=highest,
            preferred_element_type=jnp.float32,
        )
        answers[tier_index] = answer
        if tier_index > 0:
            collected[tier_index] = group_collect(answer)
    return jnp.stack(answers)[None]


def solution(mesh):
    placed = (
        P("depth", None, "rows", "shots"),
        P("depth", None, ("rows", "shots"), None),
        P("depth", None, None, None),
        P("depth", None, None, "rows"),
    )
    return jax.shard_map(
        per_device,
        mesh=mesh,
        in_specs=placed,
        out_specs=P("depth", None, "rows", "shots"),
        check_vma=False,
    )
```

profile of v0, /device:TPU:0, one launch (start us, length us, event | category | flops | bytes accessed | tf_op | source)
XLA Modules:
  0.0 194.4 jit_solution(14296305653696996673)
XLA Ops:
  7.4 0.0 all-reduce.4.cloned.1.call-start
  7.4 4.2 %fusion.6 = f32[1024,128]{1,0:T(8,128)} fusion(f32[1,2,1024,512]{3,2,1,0:T(8,128)} %param.7, f32[1,2,512,128]{3,2,1,0:T(8,128)} %param.4), kind=kOutput, calls=%fused_computation.7 | convolution fusion | flops 805306368 | bytes 2883584 | tf_op jit(solution)/shard_map/dot_general | solution.py:29
  11.5 0.0 all-reduce.4.cloned.1.call-update
  11.6 0.0 all-gather.4.cloned.1.call-start
  11.6 0.5 all-gather.4.cloned.1.call-update
  12.2 0.0 reduce-scatter.2.cloned.1.call-start
  12.2 0.7 convert_bitcast_fusion
  12.9 0.1 copy.5
  13.0 0.1 convolution_bitcast_fusion
  13.1 0.2 copy.6
  13.3 2.6 %broadcast_in_dim.11 = f32[2,512,8,128]{3,2,1,0:T(8,128)} broadcast(f32[2,512,8]{2,1,0:T(8,128)S(1)} %copy.6), dimensions={0,1,2} | broadcast | bytes 4227072 | tf_op jit(solution)/shard_map/broadcast_in_dim | solution.py:15
  15.9 4.9 %reshape.30 = f32[2,512,1024]{2,1,0:T(8,128)} reshape(f32[2,512,8,128]{3,2,1,0:T(8,128)} %broadcast_in_dim.11) | data formatting | bytes 8388608 | tf_op jit(solution)/shard_map/reshape | solution.py:15
  20.8 0.0 copy-start.1
  20.8 22.3 %all-reduce.4.cloned.1.call-done = f32[1024,128]{1,0:T(8,128)} async-done(((f32[1024,128]{1,0:T(8,128)}), f32[1024,128]{1,0:T(8,128)}) %all-reduce.4.cloned.1.call-update) | async-done | bytes 524304 | tf_op jit(solution)/shard_map/psum | solution.py:32
  43.1 46.4 %all-gather.4.cloned.1.call-done = f32[1,2,512,1024]{3,2,1,0:T(8,128)} async-done(((f32[1,2,64,1024]{3,2,1,0:T(8,128)}), f32[1,2,512,1024]{3,2,1,0:T(8,128)}) %all-gather.4.cloned.1.call-update) | async-done | bytes 4194320 | tf_op jit(solution)/shard_map/all_gather | solution.py:44
  89.5 7.7 %fusion.13 = f32[2,512,128]{2,1,0:T(8,128)} fusion(f32[2,512,1024]{2,1,0:T(8,128)} %reshape.30, f32[1,2,512,1024]{3,2,1,0:T(8,128)} %all-gather.4.cloned.1.call-done, f32[1024,128]{1,0:T(8,128)} %all-reduce.4.cloned.1.call-done), kind=kOutput, calls=%fused_computation.14 | convolution fusion | flops 1611661312 | bytes 9437184 | tf_op jit(solution)/shard_map/lgrs,lsn->grn/dot_general | solution.py:54
  97.2 0.0 reduce-scatter.2.cloned.1.call-update
  97.3 0.0 all-reduce.6.cloned.1.call-start
  97.3 6.6 %reduce-scatter.2.cloned.1.call-done = f32[1,512,128]{2,1,0:T(8,128)} async-done(((f32[2,512,128]{2,1,0:T(8,128)}), f32[1,512,128]{2,1,0:T(8,128)}) %reduce-scatter.2.cloned.1.call-update) | async-done | bytes 262160 | tf_op jit(solution)/shard_map/reduce_scatter | solution.py:19
  103.9 0.0 copy-done.1
  103.9 4.8 %fusion.15 = f32[1024,128]{0,1:T(8,128)} fusion(f32[1,2,1024,512]{3,2,1,0:T(8,128)} %param.7, f32[1,512,128]{2,1,0:T(8,128)} %reduce-scatter.2.cloned.1.call-done, f32[1,2,512,128]{3,2,1,0:T(8,128)S(1)} %copy-done.1), kind=kOutput, calls=%fused_computation.16 | convolution fusion | flops 805371904 | bytes 3145728 | tf_op jit(solution)/shard_map/dot_general | solution.py:29
  108.7 0.0 all-reduce.6.cloned.1.call-update
  108.7 0.0 all-reduce.8.cloned.1.call-start
  108.8 29.9 %all-reduce.6.cloned.1.call-done = f32[1024,128]{0,1:T(8,128)} async-done(((f32[1024,128]{0,1:T(8,128)}), f32[1024,128]{0,1:T(8,128)}) %all-reduce.6.cloned.1.call-update) | async-done | bytes 524304 | tf_op jit(solution)/shard_map/psum | solution.py:32
  138.7 3.1 %fusion = f32[128,512]{1,0:T(8,128)S(1)} fusion(f32[1024,128]{0,1:T(8,128)} %all-reduce.6.cloned.1.call-done, f32[1,2,1024,512]{3,2,1,0:T(8,128)} %param.7), kind=kOutput, calls=%fused_computation.1 | convolution fusion | flops 805306368 | bytes 2883584 | tf_op jit(solution)/shard_map/dot_general | solution.py:80
  141.7 2.4 %all-gather.1 = f32[1024,128]{0,1:T(8,128)S(1)} all-gather(f32[512,128]{0,1:T(8,128)S(1)} %bitcast.63), channel_id=3, replica_groups=mesh['depth'=2,'rows'=2,'shots'=8] {'depth'}, dimensions={0}, use_global_device_ids=true | all-gather | bytes 786432 | tf_op jit(solution)/shard_map/all_gather | solution.py:24
  144.1 0.2 copy.9
  144.3 0.0 copy-start
  144.3 10.0 %fusion.14 = f32[1024,128]{1,0:T(8,128)} fusion(f32[2,512,128]{2,1,0:T(8,128)S(1)} %bitcast.65, f32[2,512,1024]{2,1,0:T(8,128)} %reshape.30, f32[1,2,512,1024]{3,2,1,0:T(8,128)} %all-gather.4.cloned.1.call-done), kind=kOutput, calls=%fused_computation.15 | convolution fusion | flops 1611661312 | bytes 9437184 | tf_op jit(solution)/shard_map/grs,grn->sn/dot_general | solution.py:71
  154.3 0.0 all-reduce.8.cloned.1.call-update
  154.3 28.8 %all-reduce.8.cloned.1.call-done = f32[1024,128]{1,0:T(8,128)} async-done(((f32[1024,128]{1,0:T(8,128)}), f32[1024,128]{1,0:T(8,128)}) %all-reduce.8.cloned.1.call-update) | async-done | bytes 524304 | tf_op jit(solution)/shard_map/psum | solution.py:78
  183.1 0.0 copy-done
  183.1 3.2 %fusion.18 = f32[1,512,128]{1,2,0:T(8,128)S(1)} fusion(f32[1,2,1024,512]{3,2,1,0:T(8,128)} %param.7, f32[1024,128]{1,0:T(8,128)S(1)} %copy-done, f32[1024,128]{1,0:T(8,128)} %all-reduce.8.cloned.1.call-done), kind=kOutput, calls=%fused_computation.17 | convolution fusion | flops 805437440 | bytes 3407872 | tf_op jit(solution)/shard_map/dot_general | solution.py:80
  186.3 1.0 copy.7
  (2 shorter events, 0.0 us)
Async XLA Ops:
  7.4 35.7 %all-reduce.4.cloned.1.call-start = ((), (), s32[]{:S(2)}) async-start(), calls=%async_computation.1 | async-start | bytes 1048576 | tf_op jit(solution)/shard_map/psum | solution.py:32
  11.6 78.0 %all-gather.4.cloned.1.call-start = ((), (), s32[]{:S(2)}) async-start(), calls=%async_computation.5 | async-start | bytes 4718592 | tf_op jit(solution)/shard_map/all_gather | solution.py:44
  12.2 91.8 %reduce-scatter.2.cloned.1.call-start = ((), (), s32[]{:S(2)}) async-start(), calls=%async_computation.2 | async-start | bytes 786432 | tf_op jit(solution)/shard_map/reduce_scatter | solution.py:19
  20.8 83.1 %copy-start.1 = (f32[1,2,512,128]{3,2,1,0:T(8,128)S(1)}, f32[1,2,512,128]{3,2,1,0:T(8,128)}, u32[]{:S(2)}) copy-start(f32[1,2,512,128]{3,2,1,0:T(8,128)} %param.4) | copy-start | bytes 1572868
  97.3 41.4 %all-reduce.6.cloned.1.call-start = ((), (), s32[]{:S(2)}) async-start(), calls=%async_computation.3 | async-start | bytes 1048576 | tf_op jit(solution)/shard_map/psum | solution.py:32
  108.7 74.3 %all-reduce.8.cloned.1.call-start = ((), (), s32[]{:S(2)}) async-start(), calls=%async_computation.4 | async-start | bytes 1048576 | tf_op jit(solution)/shard_map/psum | solution.py:78
  144.3 38.8 %copy-start = (f32[1024,128]{1,0:T(8,128)S(1)}, f32[1024,128]{1,0:T(8,128)}, u32[]{:S(2)}) copy-start(f32[1024,128]{1,0:T(8,128)} %all-reduce.4.cloned.1.call-done) | copy-start | bytes 1572868
Sparse Core Ops, SparseCore 0:
  11.7 31.3 all-reduce.3
  97.4 6.5 reduce-scatter.1
  108.9 29.7 all-reduce.5
  154.4 28.6 all-reduce.7
Sparse Core Ops, SparseCore 1:
  14.2 75.2 all-gather.3
where the time goes:
time: 195 us; the launch traced here: 194 us
  waiting for transfers between devices  135 us (69%)
  matrix products  33 us (17%)
  between operations  14.6 us (7%)
  local copies, waits for them, and re-layouts  8.97 us (5%)
  blocking collectives  2.36 us (1%)
    psum x2, waiting for transfers between devices, invert_level(): return lax.psum(inverse_term, 'rows')  52.1 us
    all_gather x1, waiting for transfers between devices, per_device(): front_factor = lax.all_gather(factor[0], 'shots', axis=1, tiled=True)  46.4 us
    psum x1, waiting for transfers between devices, per_device(): own_columns = lax.psum(transposed, 'rows')  28.8 us
    dot_general x1, matrix products, per_device(): jnp.einsum('grs,grn->sn', factor_tiles, collected[1], precision=highest,...  9.96 us
    dot_general x2, matrix products, invert_level(): jnp.dot(inverse_block, own_rows, precision=lax.Precision.HIGHEST, preferr...  8.97 us
    dot_general x1, matrix products, per_device(): jnp.einsum('lgrs,lsn->grn', factor_tiles, lower_solved, precision=highest...  7.7 us
    reduce_scatter x1, waiting for transfers between devices, group_reduce(): lax.psum_scatter(partial_value, 'depth', scatter_dimension=0, tiled=True)  6.63 us
    dot_general x2, matrix products, per_device(): lax.dot_general(inverse_diagonal[0, tier_index], target, (((0,), (0,)), (...  6.22 us
  transfers between devices with their start and end apart: 5, of which 5 were waited for; matrix products, arithmetic and copies ran while one was open for 4% of the time, Pallas kernels for 0%

commit v1 on v0

--- a/solution.py
+++ b/solution.py
@@ -2,6 +2,7 @@
 import jax.numpy as jnp
 from jax import lax
 from jax.sharding import PartitionSpec as P
+from jax.lax import axis_index, axis_size, ppermute
 
 
 def mask_rows(factor_rows, block_mask, row_start, block_size):
@@ -41,7 +42,20 @@
     block_count = block_mask.shape[3]
     block_size = full_width // block_count
     highest = lax.Precision.HIGHEST
-    front_factor = lax.all_gather(factor[0], "shots", axis=1, tiled=True)
+
+    def use_lanes_here(matrix, lane_axis):
+        width = axis_size(lane_axis)
+        block_list = [(no, (no + 1) % width) for no in range(width)]
+
+        def time_routes_all(z_new):
+            if len(z_new) == width:
+                return z_new
+            return time_routes_all([ppermute(z_new[0], lane_axis, block_list), *z_new])
+
+        low = jnp.concatenate(time_routes_all([matrix]), axis=1)
+        return jnp.roll(low, (axis_index(lane_axis) + 1) * matrix.shape[1], axis=1)
+
+    front_factor = use_lanes_here(factor[0], "shots")
     front_count = front_factor.shape[1]
     masked = mask_rows(front_factor, block_mask, rows_index * front_count, block_size)
     solved = []

time: 195 us -> 235 us (1.21)
  waiting for transfers between devices: 135 us -> 156 us
  local copies, waits for them, and re-layouts: 8.97 us -> 26.5 us
  starting transfers between devices: 0.17 us -> 3.14 us
    ppermute x0 -> x7, waiting for transfers between devices: none -> 85.6 us  [time_routes_all(): return time_routes_all([ppermute(z_new[0], lane_axis, block_list), *z_new])]
    all_gather x1 -> x0, waiting for transfers between devices: 46.4 us -> none  [per_device(): front_factor = lax.all_gather(factor[0], 'shots', axis=1, tiled=True)]
    psum x2, waiting for transfers between devices: 52.1 us -> 33 us  [invert_level(): return lax.psum(inverse_term, 'rows')]
    unnamed x4 -> x21, local copies, waits for them, and re-layouts: 0.01 us -> 16.6 us
    ppermute x0 -> x7, starting transfers between devices: none -> 3.01 us  [time_routes_all(): return time_routes_all([ppermute(z_new[0], lane_axis, block_list), *z_new])]
  transfers between devices with their start and end apart: 5 -> 11, of which waited for: 5 -> 10; matrix products, arithmetic and copies ran while one was open for 4% -> 13% of each run, Pallas kernels for 0% -> 0%
where the time goes in v1:
time: 235 us; the launch traced here: 234 us
  waiting for transfers between devices  156 us (66%)
  matrix products  32.9 us (14%)
  local copies, waits for them, and re-layouts  26.5 us (11%)
  between operations  13.2 us (6%)
  starting transfers between devices  3.14 us (1%)
  blocking collectives  2.36 us (1%)
    ppermute x7, waiting for transfers between devices, time_routes_all(): return time_routes_all([ppermute(z_new[0], lane_axis, block_list), *z_new])  85.6 us
    psum x2, waiting for transfers between devices, invert_level(): return lax.psum(inverse_term, 'rows')  33 us
    psum x1, waiting for transfers between devices, per_device(): own_columns = lax.psum(transposed, 'rows')  28.8 us
    unnamed x21, local copies, waits for them, and re-layouts  16.6 us
    dot_general x1, matrix products, per_device(): jnp.einsum('grs,grn->sn', factor_tiles, collected[1], precision=highest,...  9.92 us
    dot_general x2, matrix products, invert_level(): jnp.dot(inverse_block, own_rows, precision=lax.Precision.HIGHEST, preferr...  8.97 us
    reduce_scatter x1, waiting for transfers between devices, group_reduce(): lax.psum_scatter(partial_value, 'depth', scatter_dimension=0, tiled=True)  8.03 us
    dot_general x1, matrix products, per_device(): jnp.einsum('lgrs,lsn->grn', factor_tiles, lower_solved, precision=highest...  7.7 us
  transfers between devices with their start and end apart: 11, of which 10 were waited for; matrix products, arithmetic and copies ran while one was open for 13% of the time, Pallas kernels for 0%

profile of v1, /device:TPU:0, one launch (start us, length us, event | category | flops | bytes accessed | tf_op | source)
XLA Modules:
  0.0 234.4 jit_solution(1825163214542470106)
XLA Ops:
  6.5 0.0 all-reduce.4.cloned.1.call-start
  6.5 3.0 %collective-permute-start = (f32[2,64,1024]{2,1,0:T(8,128)}, f32[2,64,1024]{2,1,0:T(8,128)S(1)}, u32[]{:S(2)}, u32[]{:S(2)}) collective-permute-start(f32[2,64,1024]{2,1,0:T(8,128)} %bitcast.63), channel_id=1, source_target_pairs={{0,1},{1,2},{2,3},{3,4},{4,5},{5,6},{6,7},{7,0},{8,9},{9,10},{10,1... | collective-permute-start | bytes 1572872 | tf_op jit(solution)/shard_map/ppermute | solution.py:53
  9.5 15.2 %collective-permute-done = f32[2,64,1024]{2,1,0:T(8,128)S(1)} collective-permute-done((f32[2,64,1024]{2,1,0:T(8,128)}, f32[2,64,1024]{2,1,0:T(8,128)S(1)}, u32[]{:S(2)}, u32[]{:S(2)}) %collective-permute-start) | collective-permute-done | bytes 524320 | tf_op jit(solution)/shard_map/ppermute | solution.py:53
  24.7 0.0 collective-permute-start.1
  24.7 15.8 %collective-permute-done.1 = f32[2,64,1024]{2,1,0:T(8,128)S(1)} collective-permute-done((f32[2,64,1024]{2,1,0:T(8,128)S(1)}, f32[2,64,1024]{2,1,0:T(8,128)S(1)}, u32[]{:S(2)}, u32[]{:S(2)}) %collective-permute-start.1) | collective-permute-done | bytes 524320 | tf_op jit(solution)/shard_map/ppermute | solution.py:53
  40.5 0.0 collective-permute-start.2
  40.5 14.9 %collective-permute-done.2 = f32[2,64,1024]{2,1,0:T(8,128)S(1)} collective-permute-done((f32[2,64,1024]{2,1,0:T(8,128)S(1)}, f32[2,64,1024]{2,1,0:T(8,128)S(1)}, u32[]{:S(2)}, u32[]{:S(2)}) %collective-permute-start.2) | collective-permute-done | bytes 524320 | tf_op jit(solution)/shard_map/ppermute | solution.py:53
  55.4 0.0 collective-permute-start.3
  55.4 14.1 %collective-permute-done.3 = f32[2,64,1024]{2,1,0:T(8,128)S(1)} collective-permute-done((f32[2,64,1024]{2,1,0:T(8,128)S(1)}, f32[2,64,1024]{2,1,0:T(8,128)S(1)}, u32[]{:S(2)}, u32[]{:S(2)}) %collective-permute-start.3) | collective-permute-done | bytes 524320 | tf_op jit(solution)/shard_map/ppermute | solution.py:53
  69.5 0.0 collective-permute-start.4
  69.5 13.2 %collective-permute-done.4 = f32[2,64,1024]{2,1,0:T(8,128)S(1)} collective-permute-done((f32[2,64,1024]{2,1,0:T(8,128)S(1)}, f32[2,64,1024]{2,1,0:T(8,128)S(1)}, u32[]{:S(2)}, u32[]{:S(2)}) %collective-permute-start.4) | collective-permute-done | bytes 524320 | tf_op jit(solution)/shard_map/ppermute | solution.py:53
  82.7 0.0 collective-permute-start.5
  82.7 12.5 %collective-permute-done.5 = f32[2,64,1024]{2,1,0:T(8,128)} collective-permute-done((f32[2,64,1024]{2,1,0:T(8,128)S(1)}, f32[2,64,1024]{2,1,0:T(8,128)}, u32[]{:S(2)}, u32[]{:S(2)}) %collective-permute-start.5) | collective-permute-done | bytes 524320 | tf_op jit(solution)/shard_map/ppermute | solution.py:53
  95.2 0.0 collective-permute-start.6
  95.2 4.2 %fusion.6 = f32[1024,128]{1,0:T(8,128)} fusion(f32[1,2,1024,512]{3,2,1,0:T(8,128)} %param.7, f32[1,2,512,128]{3,2,1,0:T(8,128)} %param.4), kind=kOutput, calls=%fused_computation.7 | convolution fusion | flops 805306368 | bytes 2883584 | tf_op jit(solution)/shard_map/dot_general | solution.py:30
  99.4 0.0 all-reduce.4.cloned.1.call-update
  99.4 0.0 reduce-scatter.2.cloned.1.call-start
  99.5 0.7 convert_bitcast_fusion
  100.2 0.1 copy.5
  100.3 0.1 convolution_bitcast_fusion
  100.4 0.2 copy.6
  100.6 2.6 %broadcast_in_dim.11 = f32[2,512,8,128]{3,2,1,0:T(8,128)} broadcast(f32[2,512,8]{2,1,0:T(8,128)S(1)} %copy.6), dimensions={0,1,2} | broadcast | bytes 4227072 | tf_op jit(solution)/shard_map/broadcast_in_dim | solution.py:16
  103.2 0.0 copy-start
  103.2 5.0 %reshape.30 = f32[2,512,1024]{2,1,0:T(8,128)} reshape(f32[2,512,8,128]{3,2,1,0:T(8,128)} %broadcast_in_dim.11) | data formatting | bytes 8388608 | tf_op jit(solution)/shard_map/reshape | solution.py:16
  108.2 0.0 collective-permute-done.6
  108.2 1.9 constant_dynamic-update-slice_fusion.15
  110.0 1.9 constant_dynamic-update-slice_fusion.14
  111.9 0.8 constant_dynamic-update-slice_fusion.13
  112.7 0.8 constant_dynamic-update-slice_fusion.12
  113.6 0.8 constant_dynamic-update-slice_fusion.11
  114.4 0.8 constant_dynamic-update-slice_fusion.10
  115.2 0.8 constant_dynamic-update-slice_fusion.9
  116.1 0.0 copy-done
  116.1 0.8 constant_dynamic-update-slice_fusion.8
  116.9 1.9 constant_dynamic-update-slice_fusion.7
  118.7 1.9 constant_dynamic-update-slice_fusion.6
  120.6 0.8 constant_dynamic-update-slice_fusion.5
  121.4 0.0 copy-start.2
  121.5 0.8 constant_dynamic-update-slice_fusion.4
  122.3 0.8 constant_dynamic-update-slice_fusion.3
  123.1 0.8 constant_dynamic-update-slice_fusion.2
  123.9 0.8 constant_dynamic-update-slice_fusion.1
  124.7 0.9 constant_dynamic-update-slice_fusion
  125.6 3.1 %all-reduce.4.cloned.1.call-done = f32[1024,128]{1,0:T(8,128)} async-done(((f32[1024,128]{1,0:T(8,128)}), f32[1024,128]{1,0:T(8,128)}) %all-reduce.4.cloned.1.call-update) | async-done | bytes 524304 | tf_op jit(solution)/shard_map/psum | solution.py:33
  128.8 7.7 %fusion.13 = f32[2,512,128]{2,1,0:T(8,128)} fusion(f32[2,512,1024]{2,1,0:T(8,128)} %reshape.30, f32[2,1024,1024]{2,1,0:T(8,128)} %constant_dynamic-update-slice_fusion, s32[]{:T(128)S(6)} %select_n.23, f32[1024,128]{1,0:T(8,128)} %all-reduce.4.cloned.1.call-done), kind=kOutput, calls=%fused_computation.14 | convolution fusion | flops 1611661312 | bytes 9437188 | tf_op jit(solution)/shard_map/lgrs,lsn->grn/dot_general | solution.py:68
  136.5 0.0 reduce-scatter.2.cloned.1.call-update
  136.5 0.0 all-reduce.6.cloned.1.call-start
  136.5 8.0 %reduce-scatter.2.cloned.1.call-done = f32[1,512,128]{2,1,0:T(8,128)} async-done(((f32[2,512,128]{2,1,0:T(8,128)}), f32[1,512,128]{2,1,0:T(8,128)}) %reduce-scatter.2.cloned.1.call-update) | async-done | bytes 262160 | tf_op jit(solution)/shard_map/reduce_scatter | solution.py:20
  144.6 0.0 copy-done.2
  144.6 4.8 %fusion.14 = f32[1024,128]{0,1:T(8,128)} fusion(f32[1,2,1024,512]{3,2,1,0:T(8,128)} %param.7, f32[1,512,128]{2,1,0:T(8,128)} %reduce-scatter.2.cloned.1.call-done, f32[1,2,512,128]{3,2,1,0:T(8,128)S(1)} %copy-done.2), kind=kOutput, calls=%fused_computation.15 | convolution fusion | flops 805371904 | bytes 3145728 | tf_op jit(solution)/shard_map/dot_general | solution.py:30
  149.4 0.0 copy-start.1
  149.4 0.0 all-reduce.6.cloned.1.call-update
  149.4 0.0 all-reduce.8.cloned.1.call-start
  149.4 29.9 %all-reduce.6.cloned.1.call-done = f32[1024,128]{0,1:T(8,128)} async-done(((f32[1024,128]{0,1:T(8,128)}), f32[1024,128]{0,1:T(8,128)}) %all-reduce.6.cloned.1.call-update) | async-done | bytes 524304 | tf_op jit(solution)/shard_map/psum | solution.py:33
  179.3 3.1 %fusion = f32[128,512]{1,0:T(8,128)S(1)} fusion(f32[1024,128]{0,1:T(8,128)} %all-reduce.6.cloned.1.call-done, f32[1,2,1024,512]{3,2,1,0:T(8,128)} %param.7), kind=kOutput, calls=%fused_computation.1 | convolution fusion | flops 805306368 | bytes 2883584 | tf_op jit(solution)/shard_map/dot_general | solution.py:94
  182.4 2.4 %all-gather = f32[1024,128]{0,1:T(8,128)S(1)} all-gather(f32[512,128]{0,1:T(8,128)S(1)} %bitcast.60), channel_id=2, replica_groups=mesh['depth'=2,'rows'=2,'shots'=8] {'depth'}, dimensions={0}, use_global_device_ids=true | all-gather | bytes 786432 | tf_op jit(solution)/shard_map/all_gather | solution.py:25
  184.7 0.2 copy.9
  184.9 9.9 %fusion.17 = f32[1024,128]{1,0:T(8,128)} fusion(f32[2,512,128]{2,1,0:T(8,128)S(1)} %bitcast.62, f32[2,512,1024]{2,1,0:T(8,128)} %reshape.30, f32[2,1024,1024]{2,1,0:T(8,128)} %constant_dynamic-update-slice_fusion, s32[]{:T(128)S(6)} %select_n.23), kind=kOutput, calls=%fused_computation.16 | convolution fusion | flops 1611661312 | bytes 9437188 | tf_op jit(solution)/shard_map/grs,grn->sn/dot_general | solution.py:85
  194.8 0.0 all-reduce.8.cloned.1.call-update
  194.9 28.8 %all-reduce.8.cloned.1.call-done = f32[1024,128]{1,0:T(8,128)} async-done(((f32[1024,128]{1,0:T(8,128)}), f32[1024,128]{1,0:T(8,128)}) %all-reduce.8.cloned.1.call-update) | async-done | bytes 524304 | tf_op jit(solution)/shard_map/psum | solution.py:92
  223.7 0.0 copy-done.1
  223.7 3.2 %fusion.18 = f32[1,512,128]{1,2,0:T(8,128)S(1)} fusion(f32[1,2,1024,512]{3,2,1,0:T(8,128)} %param.7, f32[1024,128]{1,0:T(8,128)S(1)} %copy-done.1, f32[1024,128]{1,0:T(8,128)} %all-reduce.8.cloned.1.call-done), kind=kOutput, calls=%fused_computation.17 | convolution fusion | flops 805437440 | bytes 3407872 | tf_op jit(solution)/shard_map/dot_general | solution.py:94
  226.9 1.0 copy.7
  (2 shorter events, 0.0 us)
Async XLA Ops:
  6.5 122.2 %all-reduce.4.cloned.1.call-start = ((), (), s32[]{:S(2)}) async-start(), calls=%async_computation.1 | async-start | bytes 1048576 | tf_op jit(solution)/shard_map/psum | solution.py:33
  6.5 18.2 %collective-permute-start = (f32[2,64,1024]{2,1,0:T(8,128)}, f32[2,64,1024]{2,1,0:T(8,128)S(1)}, u32[]{:S(2)}, u32[]{:S(2)}) collective-permute-start(f32[2,64,1024]{2,1,0:T(8,128)} %bitcast.63), channel_id=1, source_target_pairs={{0,1},{1,2},{2,3},{3,4},{4,5},{5,6},{6,7},{7,0},{8,9},{9,10},{10,1... | collective-permute-start | bytes 1572872 | tf_op jit(solution)/shard_map/ppermute | solution.py:53
  24.7 15.8 %collective-permute-start.1 = (f32[2,64,1024]{2,1,0:T(8,128)S(1)}, f32[2,64,1024]{2,1,0:T(8,128)S(1)}, u32[]{:S(2)}, u32[]{:S(2)}) collective-permute-start(f32[2,64,1024]{2,1,0:T(8,128)S(1)} %collective-permute-done), channel_id=1, source_target_pairs={{0,1},{1,2},{2,3},{3,4},{4,5},{5,6},{6,7},{7,0},{8,9},{9,10},{10,1... | collective-permute-start | bytes 1572872 | tf_op jit(solution)/shard_map/ppermute | solution.py:53
  40.5 14.9 %collective-permute-start.2 = (f32[2,64,1024]{2,1,0:T(8,128)S(1)}, f32[2,64,1024]{2,1,0:T(8,128)S(1)}, u32[]{:S(2)}, u32[]{:S(2)}) collective-permute-start(f32[2,64,1024]{2,1,0:T(8,128)S(1)} %collective-permute-done.1), channel_id=1, source_target_pairs={{0,1},{1,2},{2,3},{3,4},{4,5},{5,6},{6,7},{7,0},{8,9},{9,10},{10,1... | collective-permute-start | bytes 1572872 | tf_op jit(solution)/shard_map/ppermute | solution.py:53
  55.4 14.1 %collective-permute-start.3 = (f32[2,64,1024]{2,1,0:T(8,128)S(1)}, f32[2,64,1024]{2,1,0:T(8,128)S(1)}, u32[]{:S(2)}, u32[]{:S(2)}) collective-permute-start(f32[2,64,1024]{2,1,0:T(8,128)S(1)} %collective-permute-done.2), channel_id=1, source_target_pairs={{0,1},{1,2},{2,3},{3,4},{4,5},{5,6},{6,7},{7,0},{8,9},{9,10},{10,1... | collective-permute-start | bytes 1572872 | tf_op jit(solution)/shard_map/ppermute | solution.py:53
  69.5 13.2 %collective-permute-start.4 = (f32[2,64,1024]{2,1,0:T(8,128)S(1)}, f32[2,64,1024]{2,1,0:T(8,128)S(1)}, u32[]{:S(2)}, u32[]{:S(2)}) collective-permute-start(f32[2,64,1024]{2,1,0:T(8,128)S(1)} %collective-permute-done.3), channel_id=1, source_target_pairs={{0,1},{1,2},{2,3},{3,4},{4,5},{5,6},{6,7},{7,0},{8,9},{9,10},{10,1... | collective-permute-start | bytes 1572872 | tf_op jit(solution)/shard_map/ppermute | solution.py:53
  82.7 12.5 %collective-permute-start.5 = (f32[2,64,1024]{2,1,0:T(8,128)S(1)}, f32[2,64,1024]{2,1,0:T(8,128)}, u32[]{:S(2)}, u32[]{:S(2)}) collective-permute-start(f32[2,64,1024]{2,1,0:T(8,128)S(1)} %collective-permute-done.4), channel_id=1, source_target_pairs={{0,1},{1,2},{2,3},{3,4},{4,5},{5,6},{6,7},{7,0},{8,9},{9,10},{10,1... | collective-permute-start | bytes 1572872 | tf_op jit(solution)/shard_map/ppermute | solution.py:53
  95.2 13.0 %collective-permute-start.6 = (f32[2,64,1024]{2,1,0:T(8,128)}, f32[2,64,1024]{2,1,0:T(8,128)}, u32[]{:S(2)}, u32[]{:S(2)}) collective-permute-start(f32[2,64,1024]{2,1,0:T(8,128)} %collective-permute-done.5), channel_id=1, source_target_pairs={{0,1},{1,2},{2,3},{3,4},{4,5},{5,6},{6,7},{7,0},{8,9},{9,10},{10,1... | collective-permute-start | bytes 1572872 | tf_op jit(solution)/shard_map/ppermute | solution.py:53
  99.4 45.2 %reduce-scatter.2.cloned.1.call-start = ((), (), s32[]{:S(2)}) async-start(), calls=%async_computation.2 | async-start | bytes 786432 | tf_op jit(solution)/shard_map/reduce_scatter | solution.py:20
  103.2 12.9 %copy-start = (f32[1,2,64,1024]{3,2,1,0:T(8,128)S(1)}, f32[1,2,64,1024]{3,2,1,0:T(8,128)}, u32[]{:S(2)}) copy-start(f32[1,2,64,1024]{3,2,1,0:T(8,128)} %param.5) | copy-start | bytes 1572868
  121.4 23.1 %copy-start.2 = (f32[1,2,512,128]{3,2,1,0:T(8,128)S(1)}, f32[1,2,512,128]{3,2,1,0:T(8,128)}, u32[]{:S(2)}) copy-start(f32[1,2,512,128]{3,2,1,0:T(8,128)} %param.4) | copy-start | bytes 1572868
  136.5 42.8 %all-reduce.6.cloned.1.call-start = ((), (), s32[]{:S(2)}) async-start(), calls=%async_computation.3 | async-start | bytes 1048576 | tf_op jit(solution)/shard_map/psum | solution.py:33
  149.4 74.3 %copy-start.1 = (f32[1024,128]{1,0:T(8,128)S(1)}, f32[1024,128]{1,0:T(8,128)}, u32[]{:S(2)}) copy-start(f32[1024,128]{1,0:T(8,128)} %all-reduce.4.cloned.1.call-done) | copy-start | bytes 1572868
  149.4 74.3 %all-reduce.8.cloned.1.call-start = ((), (), s32[]{:S(2)}) async-start(), calls=%async_computation.4 | async-start | bytes 1048576 | tf_op jit(solution)/shard_map/psum | solution.py:92
Sparse Core Ops, SparseCore 0:
  99.5 29.2 all-reduce.3
  136.6 7.9 reduce-scatter.1
  149.5 29.7 all-reduce.5
  195.0 28.6 all-reduce.7
